TPU v7x, 128 devices: a whole 4x4x4 slice. The times are simulated.
128 devices in a mesh: bx: 16 (over x, z), by: 8 (over y, core).
Axes of the slice: x: 4, y: 4, z: 4, core: 2. Of those that a mesh axis runs over, the one named last changes fastest.
Arguments:
- features: bfloat16 [16, 8, 1024, 128], P('bx', 'by'), may hold values from -13 to 13
- live_count: int32 [16, 8], P('bx', 'by'), may hold values from 128 to 1024, as said below
- neighbour_map: int32 [16, 8, 27, 1024], P('bx', 'by'), may hold values from 0 to 2175, as said below
- send_rows: int32 [16, 8, 8, 128], P('bx', 'by'), may hold values from 0 to 1023, as said below
- weight: bfloat16 [3456, 128], replicated, may hold values from -0.109375 to 0.109375
- gain: float32 [128], replicated, may hold values from 0.5 to 1.5
- shift: float32 [128], replicated, may hold values from -3 to 3
- cotangent: bfloat16 [16, 8, 1024, 128], P('bx', 'by'), may hold values from -13 to 13
Outputs:
- activated: bfloat16 [16, 8, 1024, 128], P('bx', 'by')
- grad_features: bfloat16 [16, 8, 1024, 128], P('bx', 'by')
- grad_weight: float32 [27, 128, 128], P(None, 'bx', 'by')
Inputs may be any that keep to these rules, and one draw needn't show every extreme that they name: Rows 0 to live_count - 1 of a brick are live, the rest padding; in every draw some brick is full. `send_rows`: every entry is below its brick's live count; the eight blocks follow the directions (dx, dy) in row-major order with the brick's own position left out. `neighbour_map`: entries index the brick's extended table; offset 13 of a live row names that row itself; every entry of a padding row is 1536. With B = min(1024, 512) and q = r // B for a live row r, an entry below 1024 lies in rows q B to q B + B - 1, and an entry 1024 + b * 128 + h of incoming block b other than 4 has h in q * 128 B / 1024 to (q + 1) * 128 B / 1024 - 1.
All inputs are finite; a program needn't handle non-finite values.
Results may differ from a plain program's by a relative error of at most 0.029.
The roundings to bfloat16 on the way count: a program that leaves them out, or rounds other values in their place, can miss the bound.
Values may be sent and summed in bfloat16 or wider, within the bound.
No kernel may reach another device: no remote copies, remote signals or barrier semaphores. Data moves between devices by JAX's collectives and lax.ppermute only.
A program may use at most 64 MiB of HBM per device.

v0:
```python
import jax
import jax.numpy as jnp
from jax import lax
from jax.sharding import PartitionSpec as P

epsilon = 1e-05


def extended(cells, sides, width):
    for axis, dim in sides:
        count = lax.axis_size(axis)
        ends = count - 1
        head = lax.slice_in_dim(cells, 0, width, axis=dim)
        tail = lax.slice_in_dim(cells, cells.shape[dim] - width, cells.shape[dim], axis=dim)
        cells = jnp.concatenate(
            [
                lax.ppermute(tail, axis, [(i, (i + 1) % count) for i in range(ends)]),
                cells,
                lax.ppermute(head, axis, [((i + 1) % count, i) for i in range(ends)]),
            ],
            axis=dim,
        )
    return cells


def from_neighbours(outgoing):
    padded = extended(outgoing, (("bx", 0), ("by", 1)), 1)
    return padded[::2, ::2]


def per_device(features, live_count, neighbour_map, send_rows, weight, gain, shift, cotangent):
    own_rows = features[0, 0]
    rows_total, channels = own_rows.shape
    halo_rows = send_rows.shape[3]
    block_rows = min(rows_total, 512)
    blocks_count = rows_total // block_rows
    halo_window = halo_rows // blocks_count
    window_rows = block_rows + 9 * halo_window
    sent_index = send_rows[0, 0].reshape(-1)
    send_select = (
        sent_index[:, None] == lax.broadcasted_iota(jnp.int32, (1, rows_total), 1)
    ).astype(jnp.bfloat16)
    chosen_rows = jnp.dot(send_select, own_rows, preferred_element_type=jnp.float32).astype(
        jnp.bfloat16
    )
    chosen_rows = chosen_rows.reshape(8, halo_rows, channels)
    blank_block = jnp.zeros((1, halo_rows, channels), jnp.bfloat16)
    outgoing = jnp.concatenate([chosen_rows[:4], blank_block, chosen_rows[4:]], axis=0).reshape(
        3, 3, halo_rows, channels
    )
    incoming = from_neighbours(outgoing).reshape(9, blocks_count, halo_window, channels)
    index_blocks = neighbour_map[0, 0].reshape(27, blocks_count, block_rows).transpose(1, 0, 2)
    own_blocks = own_rows.reshape(blocks_count, block_rows, channels)
    halo_blocks = incoming.transpose(1, 0, 2, 3)
    block_ids = jnp.arange(blocks_count, dtype=jnp.int32)

    def selector_of(indices, block_index):
        beyond = indices - rows_total
        target = beyond // halo_rows
        inside = beyond - target * halo_rows - block_index * halo_window
        local_pos = indices - block_index * block_rows
        remote_pos = block_rows + target * halo_window + inside
        usable = (inside >= 0) & (inside < halo_window)
        position = jnp.where(indices < rows_total, local_pos, jnp.where(usable, remote_pos, -1))
        return position[:, :, None] == lax.broadcasted_iota(jnp.int32, (1, 1, window_rows), 2)

    def forward_block(pieces):
        indices, own_part, halo_part, block_index = pieces
        window = jnp.concatenate([own_part, halo_part.reshape(9 * halo_window, channels)], axis=0)
        selector = selector_of(indices, block_index).astype(jnp.bfloat16)
        gathered = jnp.einsum(
            "kbw,wc->bkc", selector, window, preferred_element_type=jnp.float32
        ).astype(jnp.bfloat16)
        columns = gathered.reshape(block_rows, 27 * channels)
        return (jnp.dot(columns, weight, preferred_element_type=jnp.float32), columns)

    conv_blocks, column_blocks = lax.map(
        forward_block, (index_blocks, own_blocks, halo_blocks, block_ids)
    )
    conv_out = conv_blocks.reshape(rows_total, channels).astype(jnp.bfloat16)
    conv_float = conv_out.astype(jnp.float32)
    live_mask = (lax.broadcasted_iota(jnp.int32, (rows_total, 1), 0) < live_count[0, 0]).astype(
        jnp.float32
    )
    local_count = jnp.sum(live_mask)
    total_sum, total_count = lax.psum(
        (jnp.sum(conv_float * live_mask, axis=0), local_count), ("bx", "by")
    )
    center = total_sum / total_count
    deviation = (conv_float - center) * live_mask
    variance = lax.psum(jnp.sum(deviation * deviation, axis=0), ("bx", "by")) / total_count
    inverse_std = lax.rsqrt(variance + epsilon)
    normalized = (conv_float - center) * inverse_std
    before = gain * normalized + shift
    activated = (jnp.maximum(before, 0.0) * live_mask).astype(jnp.bfloat16)
    upstream = cotangent[0, 0].astype(jnp.float32) * (before > 0.0) * live_mask
    sum_up, sum_cross = lax.psum(
        (jnp.sum(upstream, axis=0), jnp.sum(upstream * normalized, axis=0)), ("bx", "by")
    )
    conv_grad = (
        gain
        * inverse_std
        * (upstream - live_mask * (sum_up + normalized * sum_cross) / total_count)
    ).astype(jnp.bfloat16)
    grad_blocks = conv_grad.reshape(blocks_count, block_rows, channels)

    def backward_block(weight_acc, pieces):
        indices, columns, grad_rows, block_index = pieces
        weight_acc = weight_acc + lax.dot_general(
            columns, grad_rows, (((0,), (0,)), ((), ())), preferred_element_type=jnp.float32
        )
        column_grad = lax.dot_general(
            grad_rows, weight, (((1,), (1,)), ((), ())), preferred_element_type=jnp.float32
        )
        column_grad = column_grad.reshape(block_rows, 27, channels)
        selector = selector_of(indices, block_index).astype(jnp.float32)
        window_grad = jnp.einsum(
            "kbw,bkc->wc",
            selector,
            column_grad,
            precision=lax.Precision.HIGHEST,
            preferred_element_type=jnp.float32,
        )
        return (
            weight_acc,
            (window_grad[:block_rows], window_grad[block_rows:].reshape(9, halo_window, channels)),
        )

    start_acc = jnp.zeros((27 * channels, channels), jnp.float32)
    weight_acc, (own_parts, halo_parts) = lax.scan(
        backward_block, start_acc, (index_blocks, column_blocks, grad_blocks, block_ids)
    )
    weight_terms = weight_acc.reshape(27, channels, channels)
    partial_x = lax.psum_scatter(
        weight_terms.astype(jnp.bfloat16), "bx", scatter_dimension=1, tiled=True
    )
    summed = lax.psum_scatter(partial_x, "by", scatter_dimension=2, tiled=True).astype(jnp.float32)
    grad_weight = summed / jnp.sqrt(total_count)
    own_table = own_parts.reshape(rows_total, channels)
    halo_table = halo_parts.transpose(1, 0, 2, 3).reshape(3, 3, halo_rows, channels)
    halo_grad = halo_table.astype(jnp.bfloat16)
    returned = from_neighbours(halo_grad).reshape(9, halo_rows, channels)
    slots_back = (
        jnp.concatenate([returned[:4], returned[5:]], axis=0)
        .reshape(-1, channels)
        .astype(jnp.float32)
    )
    added_back = lax.dot_general(
        send_select.astype(jnp.float32),
        slots_back,
        (((0,), (0,)), ((), ())),
        precision=lax.Precision.HIGHEST,
        preferred_element_type=jnp.float32,
    )
    own_grad = own_table + added_back
    return (activated[None, None], own_grad.astype(jnp.bfloat16)[None, None], grad_weight)


def solution(mesh):
    return jax.shard_map(
        per_device,
        mesh=mesh,
        in_specs=(
            P("bx", "by", None, None),
            P("bx", "by"),
            P("bx", "by", None, None),
            P("bx", "by", None, None),
            P(),
            P(),
            P(),
            P("bx", "by", None, None),
        ),
        out_specs=(P("bx", "by", None, None), P("bx", "by", None, None), P(None, "bx", "by")),
        check_vma=False,
    )
```

profile of v0, /device:TPU:0, one launch (start us, length us, event | category | flops | bytes accessed | tf_op | source)
XLA Modules:
  0.0 465.1 jit_solution(409183118276341036)
XLA Ops:
  7.2 1.9 fusion.34
  9.1 3.9 collective-permute-start
  13.0 1.3 collective-permute-start.1
  15.2 4.3 collective-permute-done.1
  19.5 0.8 pad_maximum_fusion.9
  20.3 1.9 collective-permute-start.2
  22.2 1.3 collective-permute-start.3
  23.6 1.2 reduce.4
  24.7 0.1 reshape_squeeze.7
  24.9 0.6 fusion.44
  25.5 1.5 collective-permute-done.3
  27.0 1.1 pad_maximum_fusion
  28.2 38.2 %while.33 = (s32[]{:T(128)}, bf16[2,512,128]{2,1,0:T(8,128)(2,1)S(1)}, bf16[2,512,3456]{1,2,0:T(8,128)(2,1)}, bf16[2,512,128]{2,1,0:T(8,128)(2,1)}, bf16[2,9,64,...) while((s32[]{:T(128)}, ...), condition=%wide.region_1.2_spmd.clone, body=%wide.region_0.1_spmd.sunk.clone | while | flops 4321123840 | bytes 16304801 | solution.py:77
  28.2 0.6 dynamic_slice.94
  30.2 0.9 dynamic-slice_bitcast_fusion.3
  31.2 13.0 %fusion.82 = bf16[128,27,512]{2,0,1:T(8,128)(2,1)S(1)} fusion(s32[27,512]{1,0:T(8,128)S(1)} %bitcast_select_fusion.6, bf16[576,128]{1,0:T(8,128)(2,1)S(1)} %bitcast.223, bf16[512,128]{1,0:T(8,128)(2,1)S(1)} %dynamic-slice_bitcast_fusion.3), kind=kOutput, calls=%fused_computation.3.clone.1.clone | convolution fusion | flops 3867738112 | bytes 3872768 | tf_op jit(solution)/shard_map/while/body/eval_jaxpr/kbw,wc->bkc/dot_general | solution.py:71
  44.1 2.0 constant_dynamic-update-slice_fusion.6
  46.1 1.2 fusion.83
  47.3 0.6 dynamic_slice.94
  49.3 0.9 dynamic-slice_bitcast_fusion.3
  50.2 13.0 %fusion.82 = bf16[128,27,512]{2,0,1:T(8,128)(2,1)S(1)} fusion(s32[27,512]{1,0:T(8,128)S(1)} %bitcast_select_fusion.6, bf16[576,128]{1,0:T(8,128)(2,1)S(1)} %bitcast.223, bf16[512,128]{1,0:T(8,128)(2,1)S(1)} %dynamic-slice_bitcast_fusion.3), kind=kOutput, calls=%fused_computation.3.clone.1.clone | convolution fusion | flops 3867738112 | bytes 3872768 | tf_op jit(solution)/shard_map/while/body/eval_jaxpr/kbw,wc->bkc/dot_general | solution.py:71
  63.2 2.0 constant_dynamic-update-slice_fusion.6
  65.2 1.2 fusion.83
  66.4 0.2 multiply_reduce_fusion.1
  66.6 70.3 %all-reduce.2 = (f32[128]{0:T(128)S(1)}, f32[]{:T(128)}) all-reduce(f32[128]{0:T(128)S(1)} %multiply_reduce_fusion.1, f32[]{:T(128)} %fusion.44), channel_id=1, replica_groups=mesh['bx'=16,'by'=8] {'bx','by'}, use_global_device_ids=true, to_apply=%region_3.4 | all-reduce | flops 129 | bytes 1032 | tf_op jit(solution)/shard_map/psum | solution.py:86
  136.9 0.7 broadcast_divide_fusion
  137.6 0.2 multiply_reduce_fusion
  137.8 62.7 %psum.37 = f32[128]{0:T(128)S(1)} all-reduce(f32[128]{0:T(128)S(1)} %multiply_reduce_fusion), channel_id=1, replica_groups=mesh['bx'=16,'by'=8] {'bx','by'}, use_global_device_ids=true, to_apply=%region_7.8 | all-reduce | flops 128 | bytes 1024 | tf_op jit(solution)/shard_map/psum | solution.py:91
  200.5 0.7 fusion.46
  201.2 1.2 fusion.39
  202.4 64.2 %all-reduce.1 = (f32[128]{0:T(128)S(1)}, f32[128]{0:T(128)S(1)}) all-reduce(f32[128]{0:T(128)S(1)} %get-tuple-element.329, f32[128]{0:T(128)S(1)} %get-tuple-element.328), channel_id=1, replica_groups=mesh['bx'=16,'by'=8] {'bx','by'}, use_global_device_ids=true, to_apply=%region_11.12 | all-reduce | flops 256 | bytes 2048 | tf_op jit(solution)/shard_map/psum | solution.py:97
  266.6 1.9 fusion.42
  268.5 73.1 %while.34 = (s32[]{:T(128)}, f32[3456,128]{1,0:T(8,128)S(1)}, f32[2,512,128]{2,1,0:T(8,128)}, bf16[2,9,64,128]{3,2,0,1:T(8,128)(2,1)}, bf16[2,512,3456]{1,2,0:T(...) while((s32[]{:T(128)}, f32[3456,128]{1,0:T(8,128)S(1)}, ...), condition=%wide.region_13.14_spmd.clone.clone, body=%wide.region_12.13_spmd.clone.sunk.clone | while | flops 24024522752 | bytes 28413672 | solution.py:130
  268.5 0.6 dynamic_slice.99
  270.5 1.1 fusion.89
  271.6 28.7 %fusion.90 = f32[1088,128]{1,0:T(8,128)S(1)} fusion(f32[512,27,128]{2,0,1:T(8,128)S(1)} %fusion.89, s32[27,512]{1,0:T(8,128)S(1)} %bitcast_select_fusion.7), kind=kOutput, calls=%fused_computation.31.clone.1.clone | convolution fusion | flops 23117266944 | bytes 7690240 | tf_op jit(solution)/shard_map/while/body/eval_jaxpr/kbw,bkc->wc/dot_general | solution.py:117
  300.4 0.8 copy-done.4
  301.1 0.7 constant_dynamic-update-slice_fusion.7
  301.8 3.2 convolution_add_fusion.3
  305.1 0.6 dynamic_slice.99
  307.1 1.1 fusion.89
  308.2 28.7 %fusion.90 = f32[1088,128]{1,0:T(8,128)S(1)} fusion(f32[512,27,128]{2,0,1:T(8,128)S(1)} %fusion.89, s32[27,512]{1,0:T(8,128)S(1)} %bitcast_select_fusion.7), kind=kOutput, calls=%fused_computation.31.clone.1.clone | convolution fusion | flops 23117266944 | bytes 7690240 | tf_op jit(solution)/shard_map/while/body/eval_jaxpr/kbw,bkc->wc/dot_general | solution.py:117
  337.0 0.8 copy-done.4
  337.7 0.7 constant_dynamic-update-slice_fusion.7
  338.4 3.2 convolution_add_fusion.3
  341.7 1.0 convert_element_type.131
  342.8 1.0 fusion.48
  343.7 1.3 collective-permute-start.4
  345.0 1.3 collective-permute-start.5
  346.4 0.6 dynamic-slice
  348.3 4.0 collective-permute-done.5
  352.3 1.0 pad_maximum_fusion.6
  353.3 1.5 collective-permute-start.6
  354.8 1.3 collective-permute-start.7
  356.1 0.9 multiply_convert_fusion
  357.1 2.2 collective-permute-done.7
  359.3 1.1 pad_maximum_fusion.1
  360.5 64.4 %all-reduce.5.cloned.1.call-done = bf16[27,128,128]{2,1,0:T(8,128)(2,1)} async-done(((bf16[27,128,128]{2,1,0:T(8,128)(2,1)}), bf16[27,128,128]{2,1,0:T(8,128)(2,1)}) %all-reduce.5.cloned.1.call-update) | async-done | bytes 884752
  424.9 0.8 constant_dynamic-slice_fusion.1
  425.7 0.9 copy.30
  426.7 3.2 fusion.35
  429.9 27.0 %reduce-scatter.3.cloned.1.call-done = bf16[27,8,16]{0,1,2:T(8,128)(2,1)} async-done(((bf16[27,8,128]{0,1,2:T(8,128)(2,1)}), bf16[27,8,16]{0,1,2:T(8,128)(2,1)}) %reduce-scatter.3.cloned.1.call-update) | async-done | bytes 6928 | tf_op jit(solution)/shard_map/reduce_scatter | solution.py:137
  456.9 0.8 convert_divide_fusion
  457.6 0.6 copy.31
  (52 shorter events, 1.0 us)
Async XLA Ops:
  7.2 21.0 %copy-start = (bf16[3456,128]{1,0:T(8,128)(2,1)S(1)}, bf16[3456,128]{1,0:T(8,128)(2,1)}, u32[]{:S(2)}) copy-start(bf16[3456,128]{1,0:T(8,128)(2,1)} %param.16) | copy-start | bytes 2654212
  7.2 417.8 %all-reduce.5.cloned.1.call-start = ((), (), s32[]{:S(2)}) async-start(), calls=%async_computation.2 | async-start | bytes 1769472
  9.1 6.1 %collective-permute-start = (bf16[1,3,128,128]{3,2,1,0:T(8,128)(2,1)S(1)}, bf16[1,3,128,128]{3,2,1,0:T(8,128)(2,1)S(1)}, u32[]{:S(2)}, u32[]{:S(2)}) collective-permute-start(bf16[1,3,128,128]{3,2,1,0:T(8,128)(2,1)S(1)} %bitcast.239), channel_id=1, source_target_pairs={{0,8},{8,16},{16,24},{24,32},{32,40},{40,48},{48,56},{56,64},{64,7... | collective-permute-start | bytes 294920 | tf_op jit(solution)/shard_map/ppermute | solution.py:17
  13.0 6.5 %collective-permute-start.1 = (bf16[1,3,128,128]{3,2,1,0:T(8,128)(2,1)S(1)}, bf16[1,3,128,128]{3,2,1,0:T(8,128)(2,1)S(1)}, u32[]{:S(2)}, u32[]{:S(2)}) collective-permute-start(bf16[1,3,128,128]{3,2,1,0:T(8,128)(2,1)S(1)} %bitcast.238), channel_id=1, source_target_pairs={{8,0},{16,8},{24,16},{32,24},{40,32},{48,40},{56,48},{64,56},{72,6... | collective-permute-start | bytes 294920 | tf_op jit(solution)/shard_map/ppermute | solution.py:19
  20.3 5.2 %collective-permute-start.2 = (bf16[5,1,128,128]{3,2,1,0:T(8,128)(2,1)}, bf16[5,1,128,128]{3,2,1,0:T(8,128)(2,1)}, u32[]{:S(2)}, u32[]{:S(2)}) collective-permute-start(bf16[5,1,128,128]{3,2,1,0:T(8,128)(2,1)} %get-tuple-element.372), channel_id=1, source_target_pairs={{0,1},{1,2},{2,3},{3,4},{4,5},{5,6},{6,7},{8,9},{9,10},{10,11},{11... | collective-permute-start | bytes 491528 | tf_op jit(solution)/shard_map/ppermute | solution.py:17
  22.2 4.8 %collective-permute-start.3 = (bf16[5,1,128,128]{3,2,1,0:T(8,128)(2,1)}, bf16[5,1,128,128]{3,2,1,0:T(8,128)(2,1)}, u32[]{:S(2)}, u32[]{:S(2)}) collective-permute-start(bf16[5,1,128,128]{3,2,1,0:T(8,128)(2,1)} %get-tuple-element.373), channel_id=1, source_target_pairs={{1,0},{2,1},{3,2},{4,3},{5,4},{6,5},{7,6},{9,8},{10,9},{11,10},{12... | collective-permute-start | bytes 491528 | tf_op jit(solution)/shard_map/ppermute | solution.py:19
  28.2 172.3 %copy-start.1 = (f32[128]{0:T(128)S(1)}, f32[128]{0:T(128)}, u32[]{:S(2)}) copy-start(f32[128]{0:T(128)} %param.17) | copy-start | bytes 1540
  28.2 173.0 %copy-start.2 = (f32[128]{0:T(128)S(1)}, f32[128]{0:T(128)}, u32[]{:S(2)}) copy-start(f32[128]{0:T(128)} %param.18) | copy-start | bytes 1540
  268.5 77.9 %copy-start.6 = (u32[128]{0:T(128)S(1)}, u32[128]{0:T(128)}, u32[]{:S(2)}) copy-start(u32[128]{0:T(128)} %constant.182) | copy-start | bytes 1540
  271.6 28.7 %copy-start.3 = (f32[2,512,128]{2,1,0:T(8,128)S(1)}, f32[2,512,128]{2,1,0:T(8,128)}, u32[]{:S(2)}) copy-start(f32[2,512,128]{2,1,0:T(8,128)} %get-tuple-element.580) | copy-start | bytes 1572868 | tf_op jit(solution)/shard_map/while
  300.4 0.8 copy-start.4
  308.1 28.7 %copy-start.3 = (f32[2,512,128]{2,1,0:T(8,128)S(1)}, f32[2,512,128]{2,1,0:T(8,128)}, u32[]{:S(2)}) copy-start(f32[2,512,128]{2,1,0:T(8,128)} %get-tuple-element.580) | copy-start | bytes 1572868 | tf_op jit(solution)/shard_map/while
  336.9 0.8 copy-start.4
  341.6 85.0 %copy-start.5 = (s32[1,1,8,128]{3,2,1,0:T(8,128)S(1)}, s32[1,1,8,128]{3,2,1,0:T(8,128)}, u32[]{:S(2)}) copy-start(s32[1,1,8,128]{3,2,1,0:T(8,128)} %param.15) | copy-start | bytes 12292
  342.7 114.2 %reduce-scatter.3.cloned.1.call-start = ((), (), s32[]{:S(2)}) async-start(), calls=%async_computation.1 | async-start | bytes 294912 | tf_op jit(solution)/shard_map/reduce_scatter | solution.py:137
  343.7 4.6 collective-permute-start.4
  345.0 7.3 %collective-permute-start.5 = (bf16[1,3,128,128]{3,2,1,0:T(8,128)(2,1)S(1)}, bf16[1,3,128,128]{3,2,1,0:T(8,128)(2,1)S(1)}, u32[]{:S(2)}, u32[]{:S(2)}) collective-permute-start(bf16[1,3,128,128]{3,2,1,0:T(8,128)(2,1)S(1)} %bitcast.236), channel_id=1, source_target_pairs={{8,0},{16,8},{24,16},{32,24},{40,32},{48,40},{56,48},{64,56},{72,6... | collective-permute-start | bytes 294920 | tf_op jit(solution)/shard_map/ppermute | solution.py:19
  353.3 3.7 collective-permute-start.6
  354.8 4.5 collective-permute-start.7
Sparse Core Ops, SparseCore 0:
  342.8 82.0 all-reduce.4
  427.3 29.5 reduce-scatter.2
where the time goes:
time: 466 us; the launch traced here: 465 us
  blocking collectives  197 us (42%)
  waiting for transfers between devices  104 us (22%)
  matrix products  99.4 us (21%)
  between operations  16.4 us (4%)
  local copies, waits for them, and re-layouts  15.4 us (3%)
  starting transfers between devices  13.9 us (3%)
  other arithmetic  13.7 us (3%)
  loops' own time  5.44 us (1%)
    psum x1, blocking collectives, per_device(): lax.psum((jnp.sum(conv_float * live_mask, axis=0), local_count), ('bx', '...  70.3 us
    unnamed x3, waiting for transfers between devices  64.5 us
    psum x1, blocking collectives, per_device(): lax.psum((jnp.sum(upstream, axis=0), jnp.sum(upstream * normalized, axis=...  64.2 us
    psum x1, blocking collectives, per_device(): lax.psum(jnp.sum(deviation * deviation, axis=0), ('bx', 'by')) / total_count  62.7 us
    dot_general x2, matrix products, backward_block(): jnp.einsum('kbw,bkc->wc', selector, column_grad, precision=lax.Precision....  57.4 us
    reduce_scatter x1, waiting for transfers between devices, per_device(): lax.psum_scatter(partial_x, 'by', scatter_dimension=2, tiled=True)  27 us
    dot_general x2, matrix products, forward_block(): jnp.einsum('kbw,wc->bkc', selector, window, preferred_element_type=jnp.fl...  25.9 us
    ppermute x4, waiting for transfers between devices, extended(): lax.ppermute(head, axis, [((i + 1) % count, i) for i in range(ends)])  12.1 us
  transfers between devices with their start and end apart: 10, of which 6 were waited for; matrix products, arithmetic and copies ran while one was open for 2% of the time, Pallas kernels for 0%

commit v1 on v0

--- a/solution.py
+++ b/solution.py
@@ -94,8 +94,9 @@
     before = gain * normalized + shift
     activated = (jnp.maximum(before, 0.0) * live_mask).astype(jnp.bfloat16)
     upstream = cotangent[0, 0].astype(jnp.float32) * (before > 0.0) * live_mask
-    sum_up, sum_cross = lax.psum(
-        (jnp.sum(upstream, axis=0), jnp.sum(upstream * normalized, axis=0)), ("bx", "by")
+    sum_up, sum_cross = jax.lax.psum(
+        jax.lax.psum((jnp.sum(upstream, axis=0), jnp.sum(upstream * normalized, axis=0)), "by"),
+        "bx",
     )
     conv_grad = (
         gain

time: 466 us -> 451 us (0.968)
  blocking collectives: 197 us -> 184 us
    psum x1 -> x2, blocking collectives: 64.2 us -> 51 us  [the longest x1 37.1 us: per_device(): jax.lax.psum(jax.lax.psum((jnp.sum(upstream, axis=0), jnp.sum(upstream *...]
where the time goes in v1:
time: 451 us; the launch traced here: 450 us
  blocking collectives  184 us (41%)
  waiting for transfers between devices  100 us (22%)
  matrix products  99.4 us (22%)
  between operations  16.4 us (4%)
  local copies, waits for them, and re-layouts  15.5 us (3%)
  starting transfers between devices  14.9 us (3%)
  other arithmetic  13.7 us (3%)
  loops' own time  5.44 us (1%)
    psum x1, blocking collectives, per_device(): lax.psum((jnp.sum(conv_float * live_mask, axis=0), local_count), ('bx', '...  70.3 us
    psum x1, blocking collectives, per_device(): lax.psum(jnp.sum(deviation * deviation, axis=0), ('bx', 'by')) / total_count  62.7 us
    unnamed x3, waiting for transfers between devices  62.5 us
    dot_general x2, matrix products, backward_block(): jnp.einsum('kbw,bkc->wc', selector, column_grad, precision=lax.Precision....  57.4 us
    psum x1, blocking collectives, per_device(): jax.lax.psum(jax.lax.psum((jnp.sum(upstream, axis=0), jnp.sum(upstream *...  37.1 us
    reduce_scatter x1, waiting for transfers between devices, per_device(): lax.psum_scatter(partial_x, 'by', scatter_dimension=2, tiled=True)  27 us
    dot_general x2, matrix products, forward_block(): jnp.einsum('kbw,wc->bkc', selector, window, preferred_element_type=jnp.fl...  25.9 us
    psum x1, blocking collectives, per_device(): jax.lax.psum((jnp.sum(upstream, axis=0), jnp.sum(upstream * normalized, a...  13.9 us
  transfers between devices with their start and end apart: 10, of which 6 were waited for; matrix products, arithmetic and copies ran while one was open for 2% of the time, Pallas kernels for 0%

profile of v1, /device:TPU:0, one launch (start us, length us, event | category | flops | bytes accessed | tf_op | source)
XLA Modules:
  0.0 449.6 jit_solution(4440683853368022679)
XLA Ops:
  7.2 1.9 fusion.34
  9.1 3.9 collective-permute-start
  13.0 1.3 collective-permute-start.1
  15.2 4.3 collective-permute-done.1
  19.5 0.8 pad_maximum_fusion.9
  20.3 1.9 collective-permute-start.2
  22.2 1.3 collective-permute-start.3
  23.6 1.2 reduce.4
  24.9 0.6 fusion.44
  25.5 1.5 collective-permute-done.3
  27.0 1.1 pad_maximum_fusion
  28.2 38.2 %while.33 = (s32[]{:T(128)}, bf16[2,512,128]{2,1,0:T(8,128)(2,1)S(1)}, bf16[2,512,3456]{1,2,0:T(8,128)(2,1)}, bf16[2,512,128]{2,1,0:T(8,128)(2,1)}, bf16[2,9,64,...) while((s32[]{:T(128)}, ...), condition=%wide.region_1.2_spmd.clone, body=%wide.region_0.1_spmd.sunk.clone | while | flops 4321123840 | bytes 16304801 | solution.py:77
  28.2 0.6 dynamic_slice.94
  30.2 0.9 dynamic-slice_bitcast_fusion.3
  31.2 13.0 %fusion.82 = bf16[128,27,512]{2,0,1:T(8,128)(2,1)S(1)} fusion(s32[27,512]{1,0:T(8,128)S(1)} %bitcast_select_fusion.6, bf16[576,128]{1,0:T(8,128)(2,1)S(1)} %bitcast.223, bf16[512,128]{1,0:T(8,128)(2,1)S(1)} %dynamic-slice_bitcast_fusion.3), kind=kOutput, calls=%fused_computation.3.clone.1.clone | convolution fusion | flops 3867738112 | bytes 3872768 | tf_op jit(solution)/shard_map/while/body/eval_jaxpr/kbw,wc->bkc/dot_general | solution.py:71
  44.1 2.0 constant_dynamic-update-slice_fusion.6
  46.1 1.2 fusion.83
  47.3 0.6 dynamic_slice.94
  49.3 0.9 dynamic-slice_bitcast_fusion.3
  50.2 13.0 %fusion.82 = bf16[128,27,512]{2,0,1:T(8,128)(2,1)S(1)} fusion(s32[27,512]{1,0:T(8,128)S(1)} %bitcast_select_fusion.6, bf16[576,128]{1,0:T(8,128)(2,1)S(1)} %bitcast.223, bf16[512,128]{1,0:T(8,128)(2,1)S(1)} %dynamic-slice_bitcast_fusion.3), kind=kOutput, calls=%fused_computation.3.clone.1.clone | convolution fusion | flops 3867738112 | bytes 3872768 | tf_op jit(solution)/shard_map/while/body/eval_jaxpr/kbw,wc->bkc/dot_general | solution.py:71
  63.2 2.0 constant_dynamic-update-slice_fusion.6
  65.3 1.2 fusion.83
  66.4 0.2 multiply_reduce_fusion.1
  66.7 70.3 %all-reduce.1 = (f32[128]{0:T(128)S(1)}, f32[]{:T(128)}) all-reduce(f32[128]{0:T(128)S(1)} %multiply_reduce_fusion.1, f32[]{:T(128)} %fusion.44), channel_id=1, replica_groups=mesh['bx'=16,'by'=8] {'bx','by'}, use_global_device_ids=true, to_apply=%region_3.4 | all-reduce | flops 129 | bytes 1032 | tf_op jit(solution)/shard_map/psum | solution.py:86
  136.9 0.7 broadcast_divide_fusion
  137.6 0.2 multiply_reduce_fusion
  137.8 62.7 %psum.51 = f32[128]{0:T(128)S(1)} all-reduce(f32[128]{0:T(128)S(1)} %multiply_reduce_fusion), channel_id=1, replica_groups=mesh['bx'=16,'by'=8] {'bx','by'}, use_global_device_ids=true, to_apply=%region_7.8 | all-reduce | flops 128 | bytes 1024 | tf_op jit(solution)/shard_map/psum | solution.py:91
  200.5 0.7 fusion.46
  201.2 1.2 fusion.39
  202.4 13.9 %all-reduce.3 = (f32[128]{0:T(128)S(1)}, f32[128]{0:T(128)S(1)}) all-reduce(f32[128]{0:T(128)S(1)} %get-tuple-element.329, f32[128]{0:T(128)S(1)} %get-tuple-element.328), channel_id=1, replica_groups=mesh['bx'=16,'by'=8] {'by'}, use_global_device_ids=true, to_apply=%region_12.13 | all-reduce | flops 256 | bytes 2048 | tf_op jit(solution)/shard_map/psum | solution.py:98
  216.2 37.1 %all-reduce.2 = (f32[128]{0:T(128)S(1)}, f32[128]{0:T(128)S(1)}) all-reduce(f32[128]{0:T(128)S(1)} %get-tuple-element.368, f32[128]{0:T(128)S(1)} %get-tuple-element.369), channel_id=1, replica_groups=mesh['bx'=16,'by'=8] {'bx'}, use_global_device_ids=true, to_apply=%region_13.14 | all-reduce | flops 256 | bytes 2048 | tf_op jit(solution)/shard_map/psum | solution.py:97
  253.3 1.9 fusion.42
  255.2 73.2 %while.34 = (s32[]{:T(128)}, f32[3456,128]{1,0:T(8,128)S(1)}, f32[2,512,128]{2,1,0:T(8,128)}, bf16[2,9,64,128]{3,2,0,1:T(8,128)(2,1)}, bf16[2,512,3456]{1,2,0:T(...) while((s32[]{:T(128)}, f32[3456,128]{1,0:T(8,128)S(1)}, ...), condition=%wide.region_15.16_spmd.clone.clone, body=%wide.region_14.15_spmd.clone.sunk.clone | while | flops 24024522752 | bytes 28413672 | solution.py:131
  255.2 0.6 dynamic_slice.99
  257.2 1.1 fusion.89
  258.3 28.7 %fusion.90 = f32[1088,128]{1,0:T(8,128)S(1)} fusion(f32[512,27,128]{2,0,1:T(8,128)S(1)} %fusion.89, s32[27,512]{1,0:T(8,128)S(1)} %bitcast_select_fusion.7), kind=kOutput, calls=%fused_computation.31.clone.1.clone | convolution fusion | flops 23117266944 | bytes 7690240 | tf_op jit(solution)/shard_map/while/body/eval_jaxpr/kbw,bkc->wc/dot_general | solution.py:118
  287.1 0.8 copy-done.4
  287.9 0.7 constant_dynamic-update-slice_fusion.7
  288.6 3.2 convolution_add_fusion.3
  291.8 0.6 dynamic_slice.99
  293.8 1.1 fusion.89
  294.9 28.7 %fusion.90 = f32[1088,128]{1,0:T(8,128)S(1)} fusion(f32[512,27,128]{2,0,1:T(8,128)S(1)} %fusion.89, s32[27,512]{1,0:T(8,128)S(1)} %bitcast_select_fusion.7), kind=kOutput, calls=%fused_computation.31.clone.1.clone | convolution fusion | flops 23117266944 | bytes 7690240 | tf_op jit(solution)/shard_map/while/body/eval_jaxpr/kbw,bkc->wc/dot_general | solution.py:118
  323.7 0.8 copy-done.4
  324.5 0.7 constant_dynamic-update-slice_fusion.7
  325.1 3.2 convolution_add_fusion.3
  328.4 1.0 convert_element_type.131
  329.5 1.0 fusion.48
  330.5 2.5 collective-permute-start.4
  333.0 1.3 collective-permute-start.5
  334.3 0.6 dynamic-slice
  336.2 4.0 collective-permute-done.5
  340.2 1.0 pad_maximum_fusion.6
  341.2 1.3 collective-permute-start.6
  342.5 1.3 collective-permute-start.7
  343.8 0.9 multiply_convert_fusion
  344.7 1.1 collective-permute-done.7
  345.8 1.1 pad_maximum_fusion.1
  346.9 62.5 %all-reduce.6.cloned.1.call-done = bf16[27,128,128]{2,1,0:T(8,128)(2,1)} async-done(((bf16[27,128,128]{2,1,0:T(8,128)(2,1)}), bf16[27,128,128]{2,1,0:T(8,128)(2,1)}) %all-reduce.6.cloned.1.call-update) | async-done | bytes 884752
  409.4 0.8 constant_dynamic-slice_fusion.1
  410.2 0.9 copy.30
  411.2 3.2 fusion.35
  414.4 27.0 %reduce-scatter.3.cloned.1.call-done = bf16[27,8,16]{0,1,2:T(8,128)(2,1)} async-done(((bf16[27,8,128]{0,1,2:T(8,128)(2,1)}), bf16[27,8,16]{0,1,2:T(8,128)(2,1)}) %reduce-scatter.3.cloned.1.call-update) | async-done | bytes 6928 | tf_op jit(solution)/shard_map/reduce_scatter | solution.py:138
  441.4 0.8 convert_divide_fusion
  442.1 0.6 copy.31
  (53 shorter events, 1.1 us)
Async XLA Ops:
  7.2 21.0 %copy-start = (bf16[3456,128]{1,0:T(8,128)(2,1)S(1)}, bf16[3456,128]{1,0:T(8,128)(2,1)}, u32[]{:S(2)}) copy-start(bf16[3456,128]{1,0:T(8,128)(2,1)} %param.16) | copy-start | bytes 2654212
  7.2 402.3 %all-reduce.6.cloned.1.call-start = ((), (), s32[]{:S(2)}) async-start(), calls=%async_computation.2 | async-start | bytes 1769472
  9.1 6.1 %collective-permute-start = (bf16[1,3,128,128]{3,2,1,0:T(8,128)(2,1)S(1)}, bf16[1,3,128,128]{3,2,1,0:T(8,128)(2,1)S(1)}, u32[]{:S(2)}, u32[]{:S(2)}) collective-permute-start(bf16[1,3,128,128]{3,2,1,0:T(8,128)(2,1)S(1)} %bitcast.239), channel_id=1, source_target_pairs={{0,8},{8,16},{16,24},{24,32},{32,40},{40,48},{48,56},{56,64},{64,7... | collective-permute-start | bytes 294920 | tf_op jit(solution)/shard_map/ppermute | solution.py:17
  13.0 6.5 %collective-permute-start.1 = (bf16[1,3,128,128]{3,2,1,0:T(8,128)(2,1)S(1)}, bf16[1,3,128,128]{3,2,1,0:T(8,128)(2,1)S(1)}, u32[]{:S(2)}, u32[]{:S(2)}) collective-permute-start(bf16[1,3,128,128]{3,2,1,0:T(8,128)(2,1)S(1)} %bitcast.238), channel_id=1, source_target_pairs={{8,0},{16,8},{24,16},{32,24},{40,32},{48,40},{56,48},{64,56},{72,6... | collective-permute-start | bytes 294920 | tf_op jit(solution)/shard_map/ppermute | solution.py:19
  20.3 5.2 %collective-permute-start.2 = (bf16[5,1,128,128]{3,2,1,0:T(8,128)(2,1)}, bf16[5,1,128,128]{3,2,1,0:T(8,128)(2,1)}, u32[]{:S(2)}, u32[]{:S(2)}) collective-permute-start(bf16[5,1,128,128]{3,2,1,0:T(8,128)(2,1)} %get-tuple-element.374), channel_id=1, source_target_pairs={{0,1},{1,2},{2,3},{3,4},{4,5},{5,6},{6,7},{8,9},{9,10},{10,11},{11... | collective-permute-start | bytes 491528 | tf_op jit(solution)/shard_map/ppermute | solution.py:17
  22.2 4.8 %collective-permute-start.3 = (bf16[5,1,128,128]{3,2,1,0:T(8,128)(2,1)}, bf16[5,1,128,128]{3,2,1,0:T(8,128)(2,1)}, u32[]{:S(2)}, u32[]{:S(2)}) collective-permute-start(bf16[5,1,128,128]{3,2,1,0:T(8,128)(2,1)} %get-tuple-element.375), channel_id=1, source_target_pairs={{1,0},{2,1},{3,2},{4,3},{5,4},{6,5},{7,6},{9,8},{10,9},{11,10},{12... | collective-permute-start | bytes 491528 | tf_op jit(solution)/shard_map/ppermute | solution.py:19
  28.2 172.3 %copy-start.1 = (f32[128]{0:T(128)S(1)}, f32[128]{0:T(128)}, u32[]{:S(2)}) copy-start(f32[128]{0:T(128)} %param.17) | copy-start | bytes 1540
  28.2 173.0 %copy-start.2 = (f32[128]{0:T(128)S(1)}, f32[128]{0:T(128)}, u32[]{:S(2)}) copy-start(f32[128]{0:T(128)} %param.18) | copy-start | bytes 1540
  255.2 79.0 %copy-start.6 = (u32[128]{0:T(128)S(1)}, u32[128]{0:T(128)}, u32[]{:S(2)}) copy-start(u32[128]{0:T(128)} %constant.182) | copy-start | bytes 1540
  258.3 28.7 %copy-start.3 = (f32[2,512,128]{2,1,0:T(8,128)S(1)}, f32[2,512,128]{2,1,0:T(8,128)}, u32[]{:S(2)}) copy-start(f32[2,512,128]{2,1,0:T(8,128)} %get-tuple-element.582) | copy-start | bytes 1572868 | tf_op jit(solution)/shard_map/while
  287.1 0.8 copy-start.4
  294.9 28.7 %copy-start.3 = (f32[2,512,128]{2,1,0:T(8,128)S(1)}, f32[2,512,128]{2,1,0:T(8,128)}, u32[]{:S(2)}) copy-start(f32[2,512,128]{2,1,0:T(8,128)} %get-tuple-element.582) | copy-start | bytes 1572868 | tf_op jit(solution)/shard_map/while
  323.7 0.8 copy-start.4
  328.4 82.8 %copy-start.5 = (s32[1,1,8,128]{3,2,1,0:T(8,128)S(1)}, s32[1,1,8,128]{3,2,1,0:T(8,128)}, u32[]{:S(2)}) copy-start(s32[1,1,8,128]{3,2,1,0:T(8,128)} %param.15) | copy-start | bytes 12292
  329.5 111.9 %reduce-scatter.3.cloned.1.call-start = ((), (), s32[]{:S(2)}) async-start(), calls=%async_computation.1 | async-start | bytes 294912 | tf_op jit(solution)/shard_map/reduce_scatter | solution.py:138
  330.5 5.7 %collective-permute-start.4 = (bf16[1,3,128,128]{3,2,1,0:T(8,128)(2,1)S(1)}, bf16[1,3,128,128]{3,2,1,0:T(8,128)(2,1)S(1)}, u32[]{:S(2)}, u32[]{:S(2)}) collective-permute-start(bf16[1,3,128,128]{3,2,1,0:T(8,128)(2,1)S(1)} %bitcast.237), channel_id=1, source_target_pairs={{0,8},{8,16},{16,24},{24,32},{32,40},{40,48},{48,56},{56,64},{64,7... | collective-permute-start | bytes 294920 | tf_op jit(solution)/shard_map/ppermute | solution.py:17
  333.0 7.2 %collective-permute-start.5 = (bf16[1,3,128,128]{3,2,1,0:T(8,128)(2,1)S(1)}, bf16[1,3,128,128]{3,2,1,0:T(8,128)(2,1)S(1)}, u32[]{:S(2)}, u32[]{:S(2)}) collective-permute-start(bf16[1,3,128,128]{3,2,1,0:T(8,128)(2,1)S(1)} %bitcast.236), channel_id=1, source_target_pairs={{8,0},{16,8},{24,16},{32,24},{40,32},{48,40},{56,48},{64,56},{72,6... | collective-permute-start | bytes 294920 | tf_op jit(solution)/shard_map/ppermute | solution.py:19
  341.2 3.5 collective-permute-start.6
  342.5 3.3 collective-permute-start.7
Sparse Core Ops, SparseCore 0:
  329.6 79.7 all-reduce.5
  411.8 29.5 reduce-scatter.2
